TPU v7x, 256 devices: a whole 4x4x8 slice. The times are simulated.
256 devices in a mesh: rows: 4 (over y), past: 64 (over x, z, core).
Axes of the slice: x: 4, y: 4, z: 8, core: 2. Of those that a mesh axis runs over, the one named last changes fastest.
Arguments:
- tile_left: float32 [4, 64, 1024, 128], P('rows', 'past'), may hold values from -0.0625 to 0.0625
- tile_right: float32 [4, 64, 1024, 128], P('rows', 'past'), may hold values from -0.1875 to 0.1875
- diag_left: float32 [64, 1024, 128], P('past', 'rows'), may hold values from -6 to 6
- diag_right: float32 [64, 1024, 128], P('past', 'rows'), may hold values from -0.1875 to 0.1875
- present: int32 [4, 64], P('rows', 'past'), may hold values 0 or 1
- old_left: float32 [4, 1024, 128], P('rows'), may hold values from -6 to 6
- old_right: float32 [4, 1024, 128], P('rows'), may hold values from -0.1875 to 0.1875
- start: float32 [4, 1024, 128], P('rows'), may hold values from -6 to 6
Outputs:
- left: float32 [4, 1024, 128], P('rows')
- right: float32 [4, 1024, 128], P('rows')
Inputs may be any that keep to these rules, and one draw needn't show every extreme that they name: present is 1 exactly where the past tile of that tile row and panel is listed.
All inputs are finite; a program needn't handle non-finite values. No bound on the sum of `present` on one device may be relied on, other than what follows from the above.
Results may differ from a plain program's by a relative error of at most 0.00026.
Values sent between devices are 32-bit elements; how exact they have to be, the bound alone decides.
No kernel may reach another device: no remote copies, remote signals or barrier semaphores. Data moves between devices by JAX's collectives and lax.ppermute only.
A program may use at most 64 MiB of HBM per device.

v0:
```python
import math
import jax
import jax.numpy as jnp
from jax import lax
from jax.sharding import PartitionSpec as P

B = 1024
ITERS = 3
HIGH = lax.Precision.HIGHEST


def lower_inverse(gram):
    lower = jnp.linalg.cholesky(gram)
    ident = jnp.eye(gram.shape[-1], dtype=jnp.float32)
    return jax.vmap(lambda one: jax.scipy.linalg.solve_triangular(one, ident, lower=True))(lower)


def shards(tile_left, tile_right, diag_left, diag_right, present, old_left, old_right, start):
    diag_left, diag_right = (
        lax.all_gather(diag_left, "rows", axis=1, tiled=True),
        lax.all_gather(diag_right, "rows", axis=1, tiled=True),
    )
    weights = present.astype(jnp.float32)
    coupling = (
        jnp.einsum("ipbr,pbs->iprs", tile_right, diag_right, precision=HIGH)
        * weights[:, :, None, None]
    )

    def forward(block):
        inner = jnp.einsum("pbs,ibt->ipst", diag_left, block, precision=HIGH)
        middle = jnp.einsum("iprs,ipst->iprt", coupling, inner, precision=HIGH)
        summed = jnp.einsum("ipbr,iprt->ibt", tile_left, middle, precision=HIGH)
        small = jnp.einsum("ibr,ibt->irt", old_right, block, precision=HIGH)
        return (-summed, old_left, small)

    def backward(block):
        inner = jnp.einsum("ipbr,ibt->iprt", tile_left, block, precision=HIGH)
        middle = jnp.einsum("iprs,iprt->ipst", coupling, inner, precision=HIGH)
        summed = jnp.einsum("pbs,ipst->ibt", diag_left, middle, precision=HIGH)
        small = jnp.einsum("ibr,ibt->irt", old_left, block, precision=HIGH)
        return (-summed, old_right, small)

    def combine(terms, orthogonal):
        partial_value, vectors, small = terms
        total = lax.psum(partial_value, "past")
        total = total + jnp.einsum("ibr,irt->ibt", vectors, small, precision=HIGH)
        if orthogonal:
            gram = jnp.einsum("ibr,ibs->irs", total, total, precision=HIGH)
            total = jnp.einsum("ibr,isr->ibs", total, lower_inverse(gram), precision=HIGH)
        return total

    basis = combine(forward(start), True)
    for sweep in range(ITERS):
        basis = combine(forward(combine(backward(basis), True)), True)
    right = combine(backward(basis), False)
    return (basis * math.sqrt(B), right)


def solution(mesh):
    placed = (
        P("rows", "past", None, None),
        P("rows", "past", None, None),
        P("past", "rows", None),
        P("past", "rows", None),
        P("rows", "past"),
        P("rows", None, None),
        P("rows", None, None),
        P("rows", None, None),
    )
    return jax.shard_map(
        shards,
        mesh=mesh,
        in_specs=placed,
        out_specs=(P("rows", None, None), P("rows", None, None)),
        check_vma=False,
    )
```

profile of v0, /device:TPU:8, one launch (start us, length us, event | category | flops | bytes accessed | tf_op | source)
XLA Modules:
  0.0 1704.0 jit_solution(11065047977644913522)
XLA Ops:
  7.9 14.0 all_gather.7
  21.9 12.8 all_gather.6
  40.6 184.5 %all-reduce.9.cloned.1.call-done = f32[1,1024,128]{1,2,0:T(8,128)} async-done(((f32[1,1024,128]{1,2,0:T(8,128)}), f32[1,1024,128]{1,2,0:T(8,128)}) %all-reduce.9.cloned.1.call-update) | async-done | bytes 524304 | tf_op jit(solution)/shard_map/psum | solution.py:45
  225.1 1.7 fusion.9
  227.5 11.7 custom-call.18
  240.5 9.8 custom-call.19
  255.6 179.3 %all-reduce.11.cloned.1.call-done = f32[1,1024,128]{1,2,0:T(8,128)} async-done(((f32[1,1024,128]{1,2,0:T(8,128)}), f32[1,1024,128]{1,2,0:T(8,128)}) %all-reduce.11.cloned.1.call-update) | async-done | bytes 524304 | tf_op jit(solution)/shard_map/psum | solution.py:45
  435.0 1.6 fusion.11
  437.3 11.7 custom-call.20
  450.4 9.8 custom-call.21
  465.7 179.1 %all-reduce.13.cloned.1.call-done = f32[1,1024,128]{1,2,0:T(8,128)} async-done(((f32[1,1024,128]{1,2,0:T(8,128)}), f32[1,1024,128]{1,2,0:T(8,128)}) %all-reduce.13.cloned.1.call-update) | async-done | bytes 524304 | tf_op jit(solution)/shard_map/psum | solution.py:45
  644.8 1.6 fusion.13
  647.2 11.7 custom-call.22
  660.2 9.8 custom-call.23
  675.3 179.4 %all-reduce.15.cloned.1.call-done = f32[1,1024,128]{1,2,0:T(8,128)} async-done(((f32[1,1024,128]{1,2,0:T(8,128)}), f32[1,1024,128]{1,2,0:T(8,128)}) %all-reduce.15.cloned.1.call-update) | async-done | bytes 524304 | tf_op jit(solution)/shard_map/psum | solution.py:45
  854.8 1.6 fusion.15
  857.1 11.7 custom-call.24
  870.1 9.8 custom-call.25
  885.3 179.3 %all-reduce.17.cloned.1.call-done = f32[1,1024,128]{1,2,0:T(8,128)} async-done(((f32[1,1024,128]{1,2,0:T(8,128)}), f32[1,1024,128]{1,2,0:T(8,128)}) %all-reduce.17.cloned.1.call-update) | async-done | bytes 524304 | tf_op jit(solution)/shard_map/psum | solution.py:45
  1064.6 1.6 fusion.17
  1067.0 11.7 custom-call.26
  1080.0 9.8 custom-call.27
  1095.3 179.1 %all-reduce.19.cloned.1.call-done = f32[1,1024,128]{1,2,0:T(8,128)} async-done(((f32[1,1024,128]{1,2,0:T(8,128)}), f32[1,1024,128]{1,2,0:T(8,128)}) %all-reduce.19.cloned.1.call-update) | async-done | bytes 524304 | tf_op jit(solution)/shard_map/psum | solution.py:45
  1274.5 1.6 fusion.19
  1276.8 11.7 custom-call.28
  1289.9 9.8 custom-call.29
  1305.0 179.4 %all-reduce.21.cloned.1.call-done = f32[1,1024,128]{1,2,0:T(8,128)} async-done(((f32[1,1024,128]{1,2,0:T(8,128)}), f32[1,1024,128]{1,2,0:T(8,128)}) %all-reduce.21.cloned.1.call-update) | async-done | bytes 524304 | tf_op jit(solution)/shard_map/psum | solution.py:45
  1484.4 1.6 fusion.21
  1486.7 11.7 custom-call.30
  1499.8 9.8 custom-call.31
  1515.5 178.8 %all-reduce.23.cloned.1.call-done = f32[1,1024,128]{1,2,0:T(8,128)} async-done(((f32[1,1024,128]{1,2,0:T(8,128)}), f32[1,1024,128]{1,2,0:T(8,128)}) %all-reduce.23.cloned.1.call-update) | async-done | bytes 524304 | tf_op jit(solution)/shard_map/psum | solution.py:45
  1694.3 1.6 fusion.22
  (119 shorter events, 58.7 us)
Async XLA Ops:
  7.2 29.9 %copy-start = (f32[1,1,1024,128]{3,2,1,0:T(8,128)S(1)}, f32[1,1,1024,128]{3,2,1,0:T(8,128)}, u32[]{:S(2)}) copy-start(f32[1,1,1024,128]{3,2,1,0:T(8,128)} %param.11) | copy-start | bytes 1572868
  7.2 217.9 %all-reduce.9.cloned.1.call-start = ((), (), s32[]{:S(2)}) async-start(), calls=%async_computation | async-start | bytes 1048576 | tf_op jit(solution)/shard_map/psum | solution.py:45
  7.9 14.0 copy-start.5
  7.9 26.8 %copy-start.3 = (f32[1,1024,128]{2,1,0:T(8,128)S(1)}, f32[1,1024,128]{2,1,0:T(8,128)}, u32[]{:S(2)}) copy-start(f32[1,1024,128]{2,1,0:T(8,128)} %param.18) | copy-start | bytes 1572868
  34.7 1.0 copy-start.4
  38.5 1.0 copy-start.2
  38.5 186.5 %copy-start.1 = (f32[1,1024,128]{2,1,0:T(8,128)S(1)}, f32[1,1024,128]{2,1,0:T(8,128)}, u32[]{:S(2)}) copy-start(f32[1,1024,128]{2,1,0:T(8,128)} %param.16) | copy-start | bytes 1572868
  38.6 396.4 %all-reduce.11.cloned.1.call-start = ((), (), s32[]{:S(2)}) async-start(), calls=%async_computation.1 | async-start | bytes 1048576 | tf_op jit(solution)/shard_map/psum | solution.py:45
  254.4 390.4 %all-reduce.13.cloned.1.call-start = ((), (), s32[]{:S(2)}) async-start(), calls=%async_computation.2 | async-start | bytes 1048576 | tf_op jit(solution)/shard_map/psum | solution.py:45
  464.2 390.5 %all-reduce.15.cloned.1.call-start = ((), (), s32[]{:S(2)}) async-start(), calls=%async_computation.3 | async-start | bytes 1048576 | tf_op jit(solution)/shard_map/psum | solution.py:45
  674.1 390.6 %all-reduce.17.cloned.1.call-start = ((), (), s32[]{:S(2)}) async-start(), calls=%async_computation.4 | async-start | bytes 1048576 | tf_op jit(solution)/shard_map/psum | solution.py:45
  884.0 390.5 %all-reduce.19.cloned.1.call-start = ((), (), s32[]{:S(2)}) async-start(), calls=%async_computation.5 | async-start | bytes 1048576 | tf_op jit(solution)/shard_map/psum | solution.py:45
  1093.9 390.5 %all-reduce.21.cloned.1.call-start = ((), (), s32[]{:S(2)}) async-start(), calls=%async_computation.6 | async-start | bytes 1048576 | tf_op jit(solution)/shard_map/psum | solution.py:45
  1303.8 390.5 %all-reduce.23.cloned.1.call-start = ((), (), s32[]{:S(2)}) async-start(), calls=%async_computation.7 | async-start | bytes 1048576 | tf_op jit(solution)/shard_map/psum | solution.py:45
Sparse Core Ops, SparseCore 0:
  38.7 186.3 all-reduce.8
  254.5 180.4 all-reduce.10
  464.4 180.4 all-reduce.12
  674.2 180.4 all-reduce.14
  884.1 180.4 all-reduce.16
  1094.0 180.4 all-reduce.18
  1303.9 180.4 all-reduce.20
  1513.8 180.4 all-reduce.22
where the time goes:
time: 1710 us; the launch traced here: 1700 us
  waiting for transfers between devices  1440 us (84%)
  other arithmetic  161 us (9%)
  matrix products  56.9 us (3%)
  blocking collectives  26.8 us (2%)
    psum x8, waiting for transfers between devices, combine(): total = lax.psum(partial_value, 'past')  1440 us
    another operation x21, other arithmetic, lower_inverse(): lower = jnp.linalg.cholesky(gram)  86.7 us
    another operation x14, other arithmetic, lower_inverse(): jax.scipy.linalg.solve_triangular(one, ident, lower=True)  73.3 us
  transfers between devices with their start and end apart: 8, of which 8 were waited for; matrix products, arithmetic and copies ran while one was open for 1% of the time, Pallas kernels for 0%

commit v1 on v0

--- a/solution.py
+++ b/solution.py
@@ -42,7 +42,7 @@
 
     def combine(terms, orthogonal):
         partial_value, vectors, small = terms
-        total = lax.psum(partial_value, "past")
+        total = lax.all_gather(partial_value, axis_name="past").sum(axis=0)
         total = total + jnp.einsum("ibr,irt->ibt", vectors, small, precision=HIGH)
         if orthogonal:
             gram = jnp.einsum("ibr,ibs->irs", total, total, precision=HIGH)

time: 1710 us -> 1560 us (0.912)
  waiting for transfers between devices: 1440 us -> 1110 us
  local copies, waits for them, and re-layouts: 2.46 us -> 120 us
  other arithmetic: 161 us -> 236 us
    psum x8 -> x0, waiting for transfers between devices: 1440 us -> none  [combine(): total = lax.psum(partial_value, 'past')]
    all_gather x0 -> x8, waiting for transfers between devices: none -> 1110 us  [combine(): total = lax.all_gather(partial_value, axis_name='past').sum(axis=0)]
    unnamed x13 -> x11, local copies, waits for them, and re-layouts: 1.84 us -> 115 us
    reduce_sum x0 -> x8, other arithmetic: none -> 74.8 us  [combine(): total = lax.all_gather(partial_value, axis_name='past').sum(axis=0)]
where the time goes in v1:
time: 1560 us; the launch traced here: 1550 us
  waiting for transfers between devices  1110 us (71%)
  other arithmetic  236 us (15%)
  local copies, waits for them, and re-layouts  120 us (8%)
  matrix products  48.7 us (3%)
  blocking collectives  26.9 us (2%)
  between operations  16 us (1%)
    all_gather x8, waiting for transfers between devices, combine(): total = lax.all_gather(partial_value, axis_name='past').sum(axis=0)  1110 us
    unnamed x11, local copies, waits for them, and re-layouts  115 us
    another operation x21, other arithmetic, lower_inverse(): lower = jnp.linalg.cholesky(gram)  86.7 us
    reduce_sum x8, other arithmetic, combine(): total = lax.all_gather(partial_value, axis_name='past').sum(axis=0)  74.8 us
    another operation x14, other arithmetic, lower_inverse(): jax.scipy.linalg.solve_triangular(one, ident, lower=True)  73.3 us
  transfers between devices with their start and end apart: 8, of which 8 were waited for; matrix products, arithmetic and copies ran while one was open for 1% of the time, Pallas kernels for 0%

profile of v1, /device:TPU:8, one launch (start us, length us, event | category | flops | bytes accessed | tf_op | source)
XLA Modules:
  0.0 1553.2 jit_solution(2411524382220462764)
XLA Ops:
  7.9 13.9 all_gather.55
  21.8 13.0 all_gather.54
  42.9 142.4 %all-gather.17.cloned.1.call-done = f32[65536,128]{0,1:T(8,128)} async-done(((f32[1024,128]{0,1:T(8,128)}), f32[65536,128]{0,1:T(8,128)}) %all-gather.17.cloned.1.call-update) | async-done | bytes 33554448 | tf_op jit(solution)/shard_map/all_gather | solution.py:45
  185.3 28.2 %copy.74 = f32[16,8,64,1024]{3,2,1,0:T(8,128)S(1)} copy(f32[16,8,64,1024]{3,1,2,0:T(8,128)} %bitcast.353) | data formatting | bytes 67108864
  222.1 11.7 custom-call.18
  235.1 9.8 custom-call.19
  250.2 137.7 %all-gather.19.cloned.1.call-done = f32[64,1024,128]{2,1,0:T(8,128)} async-done(((f32[1,1024,128]{2,1,0:T(8,128)}), f32[64,1024,128]{2,1,0:T(8,128)}) %all-gather.19.cloned.1.call-update) | async-done | bytes 33554448 | tf_op jit(solution)/shard_map/all_gather | solution.py:45
  388.0 11.9 reduce.16
  401.4 11.7 custom-call.20
  414.4 9.8 custom-call.21
  429.4 137.7 %all-gather.21.cloned.1.call-done = f32[65536,128]{0,1:T(8,128)} async-done(((f32[1024,128]{0,1:T(8,128)}), f32[65536,128]{0,1:T(8,128)}) %all-gather.21.cloned.1.call-update) | async-done | bytes 33554448 | tf_op jit(solution)/shard_map/all_gather | solution.py:45
  567.0 28.6 %copy.75 = f32[16,8,64,1024]{3,2,1,0:T(8,128)S(1)} copy(f32[16,8,64,1024]{3,1,2,0:T(8,128)} %bitcast.350) | data formatting | bytes 67108864
  603.6 11.7 custom-call.22
  616.7 9.8 custom-call.23
  631.8 137.7 %all-gather.23.cloned.1.call-done = f32[64,1024,128]{2,1,0:T(8,128)} async-done(((f32[1,1024,128]{2,1,0:T(8,128)}), f32[64,1024,128]{2,1,0:T(8,128)}) %all-gather.23.cloned.1.call-update) | async-done | bytes 33554448 | tf_op jit(solution)/shard_map/all_gather | solution.py:45
  769.5 11.9 reduce.18
  782.9 11.7 custom-call.24
  796.0 9.8 custom-call.25
  810.9 137.7 %all-gather.25.cloned.1.call-done = f32[65536,128]{0,1:T(8,128)} async-done(((f32[1024,128]{0,1:T(8,128)}), f32[65536,128]{0,1:T(8,128)}) %all-gather.25.cloned.1.call-update) | async-done | bytes 33554448 | tf_op jit(solution)/shard_map/all_gather | solution.py:45
  948.6 28.6 %copy.76 = f32[16,8,64,1024]{3,2,1,0:T(8,128)S(1)} copy(f32[16,8,64,1024]{3,1,2,0:T(8,128)} %bitcast.351) | data formatting | bytes 67108864
  985.2 11.7 custom-call.26
  998.2 9.8 custom-call.27
  1013.4 137.7 %all-gather.27.cloned.1.call-done = f32[64,1024,128]{2,1,0:T(8,128)} async-done(((f32[1,1024,128]{2,1,0:T(8,128)}), f32[64,1024,128]{2,1,0:T(8,128)}) %all-gather.27.cloned.1.call-update) | async-done | bytes 33554448 | tf_op jit(solution)/shard_map/all_gather | solution.py:45
  1151.1 11.9 reduce.20
  1164.5 11.7 custom-call.28
  1177.5 9.8 custom-call.29
  1192.5 137.7 %all-gather.29.cloned.1.call-done = f32[65536,128]{0,1:T(8,128)} async-done(((f32[1024,128]{0,1:T(8,128)}), f32[65536,128]{0,1:T(8,128)}) %all-gather.29.cloned.1.call-update) | async-done | bytes 33554448 | tf_op jit(solution)/shard_map/all_gather | solution.py:45
  1330.1 28.2 %copy.77 = f32[16,8,64,1024]{3,2,1,0:T(8,128)S(1)} copy(f32[16,8,64,1024]{3,1,2,0:T(8,128)} %bitcast.352) | data formatting | bytes 67108864
  1366.6 11.7 custom-call.30
  1379.6 9.8 custom-call.31
  1395.5 136.9 %all-gather.31.cloned.1.call-done = f32[64,1024,128]{2,1,0:T(8,128)} async-done(((f32[1,1024,128]{2,1,0:T(8,128)}), f32[64,1024,128]{2,1,0:T(8,128)}) %all-gather.31.cloned.1.call-update) | async-done | bytes 33554448 | tf_op jit(solution)/shard_map/all_gather | solution.py:45
  1532.5 11.7 reduce.22
  (133 shorter events, 93.3 us)
Async XLA Ops:
  7.2 32.0 %copy-start = (f32[1,1,1024,128]{3,2,1,0:T(8,128)S(1)}, f32[1,1,1024,128]{3,2,1,0:T(8,128)}, u32[]{:S(2)}) copy-start(f32[1,1,1024,128]{3,2,1,0:T(8,128)} %param.11) | copy-start | bytes 1572868
  7.2 178.1 %all-gather.17.cloned.1.call-start = ((), (), s32[]{:S(2)}) async-start(), calls=%async_computation | async-start | bytes 34078720 | tf_op jit(solution)/shard_map/all_gather | solution.py:45
  40.6 347.3 %all-gather.19.cloned.1.call-start = ((), (), s32[]{:S(2)}) async-start(), calls=%async_computation.1 | async-start | bytes 34078720 | tf_op jit(solution)/shard_map/all_gather | solution.py:45
  213.5 7.2 copy-start.1
  213.5 186.5 %copy-start.2 = (f32[1,1024,128]{2,1,0:T(8,128)S(1)}, f32[1,1024,128]{2,1,0:T(8,128)}, u32[]{:S(2)}) copy-start(f32[1,1024,128]{2,1,0:T(8,128)} %param.17) | copy-start | bytes 1572868
  249.2 317.8 %all-gather.21.cloned.1.call-start = ((), (), s32[]{:S(2)}) async-start(), calls=%async_computation.2 | async-start | bytes 34078720 | tf_op jit(solution)/shard_map/all_gather | solution.py:45
  428.3 341.2 %all-gather.23.cloned.1.call-start = ((), (), s32[]{:S(2)}) async-start(), calls=%async_computation.3 | async-start | bytes 34078720 | tf_op jit(solution)/shard_map/all_gather | solution.py:45
  630.8 317.8 %all-gather.25.cloned.1.call-start = ((), (), s32[]{:S(2)}) async-start(), calls=%async_computation.4 | async-start | bytes 34078720 | tf_op jit(solution)/shard_map/all_gather | solution.py:45
  809.9 341.2 %all-gather.27.cloned.1.call-start = ((), (), s32[]{:S(2)}) async-start(), calls=%async_computation.5 | async-start | bytes 34078720 | tf_op jit(solution)/shard_map/all_gather | solution.py:45
  1012.3 317.8 %all-gather.29.cloned.1.call-start = ((), (), s32[]{:S(2)}) async-start(), calls=%async_computation.6 | async-start | bytes 34078720 | tf_op jit(solution)/shard_map/all_gather | solution.py:45
  1191.4 341.1 %all-gather.31.cloned.1.call-start = ((), (), s32[]{:S(2)}) async-start(), calls=%async_computation.7 | async-start | bytes 34078720 | tf_op jit(solution)/shard_map/all_gather | solution.py:45
Sparse Core Ops, SparseCore 0:
  40.8 144.4 all-gather.16
  249.3 138.6 all-gather.18
  428.4 138.5 all-gather.20
  630.9 138.6 all-gather.22
  810.0 138.5 all-gather.24
  1012.4 138.6 all-gather.26
  1191.5 138.5 all-gather.28
  1393.8 138.6 all-gather.30
